TPU v7x, 32 devices: a whole 2x2x4 slice. The times are simulated.
32 devices in a mesh: dp: 8 (over z, y), fsdp: 4 (over x, core).
Axes of the slice: x: 2, y: 2, z: 4, core: 2. Of those that a mesh axis runs over, the one named last changes fastest.
Arguments:
- states: bfloat16 [20480, 1280], P(('dp', 'fsdp')), may hold values from -0.1796875 to 0.1796875
- teacher: float32 [20480, 1280], P(('dp', 'fsdp')), may hold values from -0.18 to 0.18
- parent_ids: int32 [160], P('dp'), may hold values from -1 to 159, as said below
- valid_mask: int32 [20480], P(('dp', 'fsdp')), may hold values from 0 to 1, as said below
- w_query: bfloat16 [1280, 1280], P(('dp', 'fsdp')), may hold values from -0.15625 to 0.15625
- w_key: bfloat16 [1280, 1280], P(('dp', 'fsdp')), may hold values from -0.15625 to 0.15625
- w_value: bfloat16 [1280, 1280], P(('dp', 'fsdp')), may hold values from -0.15625 to 0.15625
- w_out: bfloat16 [1280, 1280], P(('dp', 'fsdp')), may hold values from -0.15625 to 0.15625
- w_up: bfloat16 [1280, 5120], P(('dp', 'fsdp')), may hold values from -0.15625 to 0.15625
- w_gate: bfloat16 [1280, 5120], P(('dp', 'fsdp')), may hold values from -0.15625 to 0.15625
- w_down: bfloat16 [5120, 1280], P(('dp', 'fsdp')), may hold values from -0.078125 to 0.078125
- qk_scale: bfloat16 [1280], P(('dp', 'fsdp')), may hold values from 0.69921875 to 1.5
- attn_rate: bfloat16 [1280], P(('dp', 'fsdp')), may hold values from 0.099609375 to 0.59765625
- mlp_rate: bfloat16 [1280], P(('dp', 'fsdp')), may hold values from 0.099609375 to 0.59765625
- up_scale: bfloat16 [5120], P(('dp', 'fsdp')), may hold values from 0.5 to 2
- gate_scale: bfloat16 [5120], P(('dp', 'fsdp')), may hold values from 0.5 to 2
Outputs:
- out_states: bfloat16 [20480, 1280], P(('dp', 'fsdp'))
- loss: float32 [], replicated
- grad_states: float32 [20480, 1280], P(('dp', 'fsdp'))
- grad_query: float32 [1280, 1280], P(('dp', 'fsdp'))
- grad_key: float32 [1280, 1280], P(('dp', 'fsdp'))
- grad_value: float32 [1280, 1280], P(('dp', 'fsdp'))
- grad_out: float32 [1280, 1280], P(('dp', 'fsdp'))
- grad_up: float32 [1280, 5120], P(('dp', 'fsdp'))
- grad_gate: float32 [1280, 5120], P(('dp', 'fsdp'))
- grad_down: float32 [5120, 1280], P(('dp', 'fsdp'))
- grad_qk_scale: float32 [1280], P(('dp', 'fsdp'))
- grad_attn_rate: float32 [1280], P(('dp', 'fsdp'))
- grad_mlp_rate: float32 [1280], P(('dp', 'fsdp'))
- grad_up_scale: float32 [5120], P(('dp', 'fsdp'))
- grad_gate_scale: float32 [5120], P(('dp', 'fsdp'))
Inputs may be any that keep to these rules, and one draw needn't show every extreme that they name: `parent_ids`: the blocks form runs of 20 in order; a parent is a block of the same run. Each run holds 1 trees of 20 blocks placed at random: a chain of 8 trunk blocks, four branch blocks whose parent is the trunk's last, and two leaf blocks under each branch; every other block has no parent. `valid_mask`: 1 on a leading part of each block, never empty, 0 after it.
All inputs are finite; a program needn't handle non-finite values.
Results may differ from a plain program's by a relative error of at most 0.017.
Values may be sent and summed in bfloat16 or wider, within the bound.
A program may use at most 576 MiB of HBM per device.

v0:
```python
import math
import jax
import jax.numpy as jnp
from jax import lax
from jax.sharding import PartitionSpec as P

D = 1280
HEADS = 20
HEAD_DIM = 64
FF = 5120
BLOCK = 128
DEPTH = 10
EPS = 1e-06


def unit_rows(vector):
    inverse = lax.rsqrt(jnp.sum(vector * vector, axis=-1, keepdims=True) + EPS)
    return (vector * inverse, inverse)


def unit_back(grad, unit, inverse):
    return (grad - unit * jnp.sum(grad * unit, axis=-1, keepdims=True)) * inverse


def project(left, right):
    return jnp.dot(left, right, preferred_element_type=jnp.float32)


def project_back(grad, weight):
    return jnp.einsum("te,de->td", grad, weight, preferred_element_type=jnp.float32)


def ancestors(local_parent):
    column = jnp.arange(local_parent.shape[0], dtype=jnp.int32)
    columns = [column]
    for depth_step in range(DEPTH - 1):
        column = jnp.where(column >= 0, local_parent[jnp.maximum(column, 0)], -1)
        columns.append(column)
    return jnp.stack(columns, axis=1)


def head_back(grad_flat, unit, inverse, scale):
    scaled = (grad_flat * scale).reshape(unit.shape)
    raw = unit_back(scaled, unit, inverse).reshape(grad_flat.shape)
    scale_grad = jnp.sum(grad_flat * unit.reshape(grad_flat.shape), axis=0)
    return (raw, scale_grad)


def local(
    states,
    teacher,
    parent_ids,
    valid_mask,
    w_query,
    w_key,
    w_value,
    w_out,
    w_up,
    w_gate,
    w_down,
    qk_scale,
    attn_rate,
    mlp_rate,
    up_scale,
    gate_scale,
):
    rows_dev = states.shape[0]
    blocks_dev = rows_dev // BLOCK
    width_rows = w_query.shape[0]
    span = DEPTH * BLOCK
    factor = math.sqrt(HEAD_DIM)
    root_width = math.sqrt(D)
    mask_f = valid_mask.astype(jnp.float32)
    qkv_local = jnp.concatenate((w_query, w_key, w_value), axis=1)
    scal_width_local = jnp.stack((qk_scale, attn_rate, mlp_rate), axis=1)
    piece_qkv = lax.all_gather(qkv_local, ("dp", "fsdp"), axis=0, tiled=True)
    piece_out = lax.all_gather(w_out, ("dp", "fsdp"), axis=0, tiled=True)
    piece_scal = lax.all_gather(scal_width_local, ("dp", "fsdp"), axis=0, tiled=True)
    lefts = states
    total = jnp.dot(lefts, piece_qkv, preferred_element_type=jnp.float32)
    scal_whole = piece_scal
    qkv_raw = total
    scal_width = scal_whole
    scale_qk = scal_width[:, 0].astype(jnp.float32)
    rate_attn = scal_width[:, 1].astype(jnp.float32)
    rate_mlp = scal_width[:, 2].astype(jnp.float32)
    query_raw = qkv_raw[:, :D]
    key_raw = qkv_raw[:, D : 2 * D]
    values = qkv_raw[:, 2 * D :].astype(jnp.bfloat16)
    query_unit, query_inv = unit_rows(query_raw.reshape(rows_dev, HEADS, HEAD_DIM))
    key_unit, key_inv = unit_rows(key_raw.reshape(rows_dev, HEADS, HEAD_DIM))
    query_n = (query_unit.reshape(rows_dev, D) * scale_qk).astype(jnp.bfloat16)
    key_n = (key_unit.reshape(rows_dev, D) * scale_qk).astype(jnp.bfloat16)
    key_group, value_group = (
        lax.all_gather(key_n, "fsdp", axis=0, tiled=True),
        lax.all_gather(values, "fsdp", axis=0, tiled=True),
    )
    group_blocks = parent_ids.shape[0]
    group_base = lax.axis_index("dp") * group_blocks
    local_parent = jnp.where(parent_ids >= 0, parent_ids - group_base, -1)
    paths_all = ancestors(local_parent)
    own_first = lax.axis_index("fsdp") * blocks_dev
    paths = lax.dynamic_slice_in_dim(paths_all, own_first, blocks_dev, 0)
    safe_paths = jnp.maximum(paths, 0)
    key_rows = key_group.reshape(group_blocks, BLOCK, D)[safe_paths].reshape(
        blocks_dev, span, HEADS, HEAD_DIM
    )
    value_rows = value_group.reshape(group_blocks, BLOCK, D)[safe_paths].reshape(
        blocks_dev, span, HEADS, HEAD_DIM
    )
    slot_of = jnp.arange(span, dtype=jnp.int32) // BLOCK
    offset = jnp.arange(span, dtype=jnp.int32) % BLOCK
    row_pos = jnp.arange(BLOCK, dtype=jnp.int32)
    causal = offset[None, :] <= row_pos[:, None]
    is_live = jnp.take(paths, slot_of, axis=1) >= 0
    allowed = jnp.where(slot_of[None, None, :] == 0, causal[None], is_live[:, None, :])[:, None]
    query_heads = query_n.reshape(blocks_dev, BLOCK, HEADS, HEAD_DIM)
    scores = factor * jnp.einsum(
        "bqhd,bkhd->bhqk", query_heads, key_rows, preferred_element_type=jnp.float32
    )
    scores = jnp.where(allowed, scores, jnp.float32(-1e30))
    row_max = jnp.max(scores, axis=-1, keepdims=True)
    powers = jnp.exp(scores - row_max)
    row_sum = jnp.sum(powers, axis=-1, keepdims=True)
    probs_b = (powers / row_sum).astype(jnp.bfloat16)
    log_total = row_max + jnp.log(row_sum)
    mixed = jnp.einsum("bhqk,bkhd->bqhd", probs_b, value_rows, preferred_element_type=jnp.float32)
    mixed = mixed.reshape(rows_dev, D).astype(jnp.bfloat16)
    inputs = states.astype(jnp.float32)
    attn = project(mixed, piece_out)
    attn_unit, attn_inv = unit_rows(attn)
    hidden, hidden_inv = unit_rows(inputs + rate_attn * (attn_unit - inputs))
    hidden_b = hidden.astype(jnp.bfloat16)
    ffn_local = jnp.concatenate((w_up, w_gate), axis=1)
    scal_hidden_local = jnp.concatenate(
        (up_scale.reshape(width_rows, 4), gate_scale.reshape(width_rows, 4)), axis=1
    )
    piece_ffn = lax.all_gather(ffn_local, ("dp", "fsdp"), axis=0, tiled=True)
    piece_scal = lax.all_gather(scal_hidden_local, ("dp", "fsdp"), axis=0, tiled=True)
    lefts = hidden_b
    total = jnp.dot(lefts, piece_ffn, preferred_element_type=jnp.float32)
    scal_whole = piece_scal
    scale_up = scal_whole[:, :4].reshape(FF).astype(jnp.float32)
    scale_gate = scal_whole[:, 4:].reshape(FF).astype(jnp.float32)
    up_proj = total[:, :FF]
    gate_proj = total[:, FF:]
    upscaled = up_proj * scale_up
    gated = gate_proj * scale_gate * root_width
    sigmoid_gate = jax.nn.sigmoid(gated)
    act = (upscaled * (gated * sigmoid_gate)).astype(jnp.bfloat16)
    lefts = act
    down = jnp.dot(
        lefts,
        lax.all_gather(w_down, ("dp", "fsdp"), axis=0, tiled=True),
        preferred_element_type=jnp.float32,
    )
    down_unit, down_inv = unit_rows(down)
    result, result_inv = unit_rows(hidden + rate_mlp * (down_unit - hidden))
    loss_local = jnp.sum(mask_f[:, None] * (result - teacher) ** 2)
    valid_count, loss_sum = lax.psum((jnp.sum(mask_f), loss_local), ("dp", "fsdp"))
    loss = loss_sum / valid_count
    g_result = 2.0 * mask_f[:, None] * (result - teacher) / valid_count
    g_last = unit_back(g_result, result, result_inv)
    g_hidden = g_last * (1.0 - rate_mlp)
    g_rate_mlp = jnp.sum(g_last * (down_unit - hidden), axis=0)
    g_down = unit_back(g_last * rate_mlp, down_unit, down_inv).astype(jnp.bfloat16)
    g_act = jnp.einsum(
        "te,fe->tf",
        g_down,
        lax.all_gather(w_down, ("dp", "fsdp"), axis=0, tiled=True),
        preferred_element_type=jnp.float32,
    )
    g_upscaled = g_act * (gated * sigmoid_gate)
    g_gated = g_act * upscaled * sigmoid_gate * (1.0 + gated * (1.0 - sigmoid_gate))
    grad_up_scale = jnp.sum(g_upscaled * up_proj, axis=0)
    grad_gate_scale = jnp.sum(g_gated * gate_proj * root_width, axis=0)
    g_up = (g_upscaled * scale_up).astype(jnp.bfloat16)
    g_gate = (g_gated * scale_gate * root_width).astype(jnp.bfloat16)
    g_both = jnp.concatenate((g_up, g_gate), axis=1)
    g_hidden = g_hidden + jnp.einsum(
        "tc,dc->td",
        g_both,
        lax.all_gather(ffn_local, ("dp", "fsdp"), axis=0, tiled=True),
        preferred_element_type=jnp.float32,
    )
    scal_terms = jnp.concatenate(
        (grad_up_scale.reshape(D, 4), grad_gate_scale.reshape(D, 4)), axis=1
    )
    lefts = hidden_b
    main = jnp.einsum("td,tc->dc", lefts, g_both, preferred_element_type=jnp.float32)
    ffn_share = lax.psum_scatter(
        jnp.concatenate((main, scal_terms), axis=1), ("dp", "fsdp"), scatter_dimension=0, tiled=True
    )
    lefts = act
    grad_down = lax.psum_scatter(
        jnp.einsum("tf,te->fe", lefts, g_down, preferred_element_type=jnp.float32),
        ("dp", "fsdp"),
        scatter_dimension=0,
        tiled=True,
    )
    g_pre = unit_back(g_hidden, hidden, hidden_inv)
    g_states = g_pre * (1.0 - rate_attn)
    g_rate_attn = jnp.sum(g_pre * (attn_unit - inputs), axis=0)
    g_attn = unit_back(g_pre * rate_attn, attn_unit, attn_inv).astype(jnp.bfloat16)
    g_mixed = project_back(g_attn, piece_out).astype(jnp.bfloat16)
    scores = factor * jnp.einsum(
        "bqhd,bkhd->bhqk", query_heads, key_rows, preferred_element_type=jnp.float32
    )
    probs = jnp.where(allowed, jnp.exp(scores - log_total), jnp.float32(0.0))
    probs_again = probs.astype(jnp.bfloat16)
    g_heads = g_mixed.reshape(blocks_dev, BLOCK, HEADS, HEAD_DIM)
    g_probs = jnp.einsum("bqhd,bkhd->bhqk", g_heads, value_rows, preferred_element_type=jnp.float32)
    delta = jnp.sum(probs * g_probs, axis=-1, keepdims=True)
    g_scores = (probs * (g_probs - delta)).astype(jnp.bfloat16)
    g_query_n = factor * jnp.einsum(
        "bhqk,bkhd->bqhd", g_scores, key_rows, preferred_element_type=jnp.float32
    )
    g_key_rows = factor * jnp.einsum(
        "bhqk,bqhd->bkhd", g_scores, query_heads, preferred_element_type=jnp.float32
    )
    g_value_rows = jnp.einsum(
        "bhqk,bqhd->bkhd", probs_again, g_heads, preferred_element_type=jnp.float32
    )
    flat_paths = safe_paths.reshape(blocks_dev * DEPTH)
    g_key_group = (
        jnp.zeros((group_blocks, BLOCK, D), jnp.float32)
        .at[flat_paths]
        .add(g_key_rows.reshape(blocks_dev * DEPTH, BLOCK, D))
    )
    g_value_group = (
        jnp.zeros((group_blocks, BLOCK, D), jnp.float32)
        .at[flat_paths]
        .add(g_value_rows.reshape(blocks_dev * DEPTH, BLOCK, D))
    )
    g_key_n, g_values = (
        lax.psum_scatter(
            g_key_group.reshape(group_blocks * BLOCK, D).astype(jnp.bfloat16),
            "fsdp",
            scatter_dimension=0,
            tiled=True,
        ).astype(jnp.float32),
        lax.psum_scatter(
            g_value_group.reshape(group_blocks * BLOCK, D).astype(jnp.bfloat16),
            "fsdp",
            scatter_dimension=0,
            tiled=True,
        ).astype(jnp.float32),
    )
    g_query_raw, scale_from_query = head_back(
        g_query_n.reshape(rows_dev, D), query_unit, query_inv, scale_qk
    )
    g_key_raw, scale_from_key = head_back(g_key_n, key_unit, key_inv, scale_qk)
    grad_qk_scale = scale_from_query + scale_from_key
    g_qkv = jnp.concatenate(
        (
            g_query_raw.astype(jnp.bfloat16),
            g_key_raw.astype(jnp.bfloat16),
            g_values.astype(jnp.bfloat16),
        ),
        axis=1,
    )
    g_states = g_states + jnp.einsum(
        "tc,dc->td",
        g_qkv,
        lax.all_gather(qkv_local, ("dp", "fsdp"), axis=0, tiled=True),
        preferred_element_type=jnp.float32,
    )
    vector_terms = jnp.stack((grad_qk_scale, g_rate_attn, g_rate_mlp), axis=1)
    lefts = states
    main = jnp.einsum("td,tc->dc", lefts, g_qkv, preferred_element_type=jnp.float32)
    outer = jnp.einsum("td,tc->dc", mixed, g_attn, preferred_element_type=jnp.float32)
    attn_share = lax.psum_scatter(
        jnp.concatenate((main, outer, vector_terms), axis=1),
        ("dp", "fsdp"),
        scatter_dimension=0,
        tiled=True,
    )
    return (
        result.astype(jnp.bfloat16),
        loss,
        g_states,
        attn_share[:, :D],
        attn_share[:, D : 2 * D],
        attn_share[:, 2 * D : 3 * D],
        attn_share[:, 3 * D : 4 * D],
        ffn_share[:, :FF],
        ffn_share[:, FF : 2 * FF],
        grad_down,
        attn_share[:, 4 * D],
        attn_share[:, 4 * D + 1],
        attn_share[:, 4 * D + 2],
        ffn_share[:, 2 * FF : 2 * FF + 4].reshape(-1),
        ffn_share[:, 2 * FF + 4 : 2 * FF + 8].reshape(-1),
    )


def solution(mesh):
    placed = (
        P(("dp", "fsdp"), None),
        P(("dp", "fsdp"), None),
        P("dp"),
        P(("dp", "fsdp")),
        P(("dp", "fsdp"), None),
        P(("dp", "fsdp"), None),
        P(("dp", "fsdp"), None),
        P(("dp", "fsdp"), None),
        P(("dp", "fsdp"), None),
        P(("dp", "fsdp"), None),
        P(("dp", "fsdp"), None),
        P(("dp", "fsdp")),
        P(("dp", "fsdp")),
        P(("dp", "fsdp")),
        P(("dp", "fsdp")),
        P(("dp", "fsdp")),
    )
    return jax.shard_map(
        local,
        mesh=mesh,
        in_specs=placed,
        out_specs=(
            P(("dp", "fsdp"), None),
            P(),
            P(("dp", "fsdp"), None),
            P(("dp", "fsdp"), None),
            P(("dp", "fsdp"), None),
            P(("dp", "fsdp"), None),
            P(("dp", "fsdp"), None),
            P(("dp", "fsdp"), None),
            P(("dp", "fsdp"), None),
            P(("dp", "fsdp"), None),
            P(("dp", "fsdp")),
            P(("dp", "fsdp")),
            P(("dp", "fsdp")),
            P(("dp", "fsdp")),
            P(("dp", "fsdp")),
        ),
        check_vma=False,
    )
```

profile of v0, /device:TPU:14, one launch (start us, length us, event | category | flops | bytes accessed | tf_op | source)
XLA Modules:
  0.0 2938.8 jit_solution(9725263483345402264)
XLA Ops:
  9.0 86.4 %all-gather.9.cloned.1.call-done = bf16[1280,3840]{1,0:T(8,128)(2,1)} async-done(((bf16[40,3840]{1,0:T(8,128)(2,1)}), bf16[1280,3840]{1,0:T(8,128)(2,1)}) %all-gather.9.cloned.1.call-update) | async-done | bytes 9830416 | tf_op jit(solution)/shard_map/all_gather | solution.py:76
  95.4 11.2 convolution_bitcast_fusion.1
  106.6 3.8 copy-done.2
  111.9 29.3 all-gather
  141.9 5.1 slice_multiply_fusion.1
  147.1 3.4 reduce_sum.198
  150.9 6.5 multiply_convert_fusion.7
  173.8 38.1 %all-gather.1 = bf16[32,40,8]{1,2,0:T(8,128)(2,1)S(1)} all-gather(bf16[1,40,8]{1,2,0:T(8,128)(2,1)S(1)} %maximum_bitcast_fusion), channel_id=1, replica_groups=mesh['dp'=8,'fsdp'=4] {'dp','fsdp'}, dimensions={0}, use_global_device_ids=true | all-gather | bytes 21120 | tf_op jit(solution)/shard_map/all_gather | solution.py:139
  214.5 50.4 %psum.15 = f32[]{:T(128)} all-reduce(f32[]{:T(128)} %get-tuple-element.167), channel_id=1, replica_groups=mesh['dp'=8,'fsdp'=4] {'dp','fsdp'}, use_global_device_ids=true, to_apply=%region_11.12 | all-reduce | flops 1 | bytes 8 | tf_op jit(solution)/shard_map/psum | solution.py:160
  266.3 3.8 reshape.781
  270.1 9.9 copy.194
  280.0 10.6 gather_fusion.9
  290.6 46.2 %reshape.933 = bf16[5,1280,20,64]{3,2,1,0:T(8,128)(2,1)} reshape(bf16[50,128,1280]{2,1,0:T(8,128)(2,1)} %gather_fusion.9) | data formatting | bytes 32768000 | tf_op jit(solution)/shard_map/reshape | solution.py:108
  336.8 47.0 %copy.213 = bf16[5,1280,20,64]{1,3,2,0:T(8,128)(2,1)} copy(bf16[5,1280,20,64]{3,2,1,0:T(8,128)(2,1)} %reshape.933) | data formatting | bytes 32768000 | tf_op jit(solution)/shard_map/reshape | solution.py:108
  383.8 9.5 copy.209
  393.3 10.7 gather_fusion.11
  404.0 46.3 %reshape.934 = bf16[5,1280,20,64]{3,2,1,0:T(8,128)(2,1)} reshape(bf16[50,128,1280]{2,1,0:T(8,128)(2,1)} %gather_fusion.11) | data formatting | bytes 32768000 | tf_op jit(solution)/shard_map/reshape | solution.py:105
  450.4 47.0 %copy.212 = bf16[5,1280,20,64]{1,3,2,0:T(8,128)(2,1)} copy(bf16[5,1280,20,64]{3,2,1,0:T(8,128)(2,1)} %reshape.934) | data formatting | bytes 32768000 | tf_op jit(solution)/shard_map/reshape | solution.py:105
  497.3 30.2 %select_reduce_fusion = (f32[5,20,128]{2,1,0:T(8,128)S(1)}, f32[5,20,128,1280]{3,2,1,0:T(8,128)}) fusion(pred[5,128,1280]{2,1,0:T(8,128)(4,1)S(1)} %broadcast_select_fusion, bf16[5,1280,20,64]{1,3,2,0:T(8,128)(2,1)} %copy.212, bf16[5,128,20,64]{1,0,3,2:T(8,128)(2,1)S(1)} %reshape.781), kind=kOutput, calls=%fused_computation.20 | convolution fusion | flops 2146291200 | bytes 84428800 | tf_op jit(solution)/shard_map/bqhd,bkhd->bhqk/dot_general | solution.py:118
  527.5 21.3 fusion.1
  548.8 31.6 %fusion.32 = bf16[5,128,20,64]{1,3,2,0:T(8,128)(2,1)} fusion(bf16[5,1280,20,64]{1,3,2,0:T(8,128)(2,1)} %copy.213, f32[5,20,128,1280]{3,2,1,0:T(8,128)} %get-tuple-element.169, f32[5,20,128]{2,1,0:T(8,128)S(1)} %fusion.1, f32[5,20,128]{2,1,0:T(8,128)S(1)} %get-tuple-element.168, pred[5,128,1280]{2,1,0:T(8,128)(4,1)S(1)} %broadcast_select_fusion), kind=kOutput, calls=%fused_computation.107 | convolution fusion | flops 2179891200 | bytes 84480000 | tf_op jit(solution)/shard_map/bhqk,bkhd->bqhd/dot_general | solution.py:127
  583.3 5.3 multiply_reduce_fusion.14
  591.0 27.2 fusion.63
  618.3 12.6 multiply_convert_fusion.3
  630.8 13.2 multiply_reduce_fusion.12
  646.0 2.9 multiply_reduce_fusion.9
  648.9 4.6 multiply_reduce_fusion.3
  656.0 29.7 %multiply_reduce_fusion.1 = (f32[5120]{0:T(1024)}, f32[5120]{0:T(1024)}, f32[640,5120]{1,0:T(8,128)}, bf16[640,5120]{1,0:T(8,128)(2,1)}) fusion(f32[640,10240]{1,0:T(8,128)} %fusion.63, f32[5120]{0:T(1024)S(1)} %copy-done.40, f32[5120]{0:T(1024)S(1)} %copy-done.43, bf16[640,1280]{1,0:T(8,128)(2,1)S(1)} %multiply_convert_fusion.5, ...), kind=kOutput, calls=%fused_computation.33 | convolution fusion | flops 8457410560 | bytes 60702720 | tf_op jit(solution)/shard_map/te,fe->tf/dot_general | solution.py:167
  685.7 9.2 multiply_convert_fusion.1
  694.9 26.7 multiply_reduce_fusion.7
  721.6 5.6 multiply_reduce_fusion.4
  733.2 4.3 reshape.935
  737.6 4.6 copy.221
  742.2 55.0 %multiply_reduce_fusion = (f32[5,20,128]{2,1,0:T(8,128)}, f32[5,20,128,1280]{3,2,1,0:T(8,128)}) fusion(f32[5,20,128,1280]{3,2,1,0:T(8,128)} %get-tuple-element.169, f32[5,20,128]{2,1,0:T(8,128)S(1)} %copy-done.32, pred[5,128,1280]{2,1,0:T(8,128)(4,1)S(1)} %copy-done.6, bf16[5,128,20,64]{1,3,2,0:T(8,128)(2,1)S(1)} %copy.221, bf16[5,1280,20,64]{1,3,2,0:T(8,128)(2,1)} %copy.213), kind=kOutput, calls=%fused_computation.16 | convolution fusion | flops 2179059200 | bytes 150016000 | tf_op jit(solution)/shard_map/bqhd,bkhd->bhqk/dot_general | solution.py:212
  797.1 52.9 %multiply_convert_fusion = bf16[5,20,128,1280]{3,2,1,0:T(8,128)(2,1)} fusion(f32[5,20,128,1280]{3,2,1,0:T(8,128)} %get-tuple-element.177, f32[5,20,128,1280]{3,2,1,0:T(8,128)} %get-tuple-element.169, f32[5,20,128]{2,1,0:T(8,128)} %get-tuple-element.176, f32[5,20,128]{2,1,0:T(8,128)S(1)} %copy-done.32, pred[5,128,1280]{2,1,0:T(8,128)(4,1)S(1)} %copy-done.6), kind=kLoop, calls=%fused_computation.15 | loop fusion | flops 98304000 | bytes 164761600 | tf_op jit(solution)/shard_map/convert_element_type | solution.py:214
  850.1 20.9 multiply_bitcast_fusion
  871.0 53.4 %copy.240 = f32[5,1280,20,64]{3,2,1,0:T(8,128)} copy(f32[5,1280,20,64]{1,3,2,0:T(8,128)} %multiply_bitcast_fusion) | data formatting | bytes 65536000 | tf_op jit(solution)/shard_map/reshape | solution.py:228
  924.4 57.4 %reshape.925 = f32[50,128,1280]{2,1,0:T(8,128)} reshape(f32[5,1280,20,64]{3,2,1,0:T(8,128)} %copy.240) | data formatting | bytes 65536000 | tf_op jit(solution)/shard_map/reshape | solution.py:228
  981.8 6.1 broadcast.941.clone.1
  987.9 65.4 %scatter_fusion = f32[20,128,1280]{2,1,0:T(8,128)} fusion(f32[20,128,1280]{2,1,0:T(8,128)} %broadcast.941.clone.1, s32[50]{0:T(128)S(1)} %copy-done.55, f32[50,128,1280]{2,1,0:T(8,128)} %reshape.925), kind=kCustom, calls=%fused_computation.12 | custom fusion | flops 8192000 | bytes 98304200 | tf_op jit(solution)/shard_map/scatter-add | solution.py:228
  1053.2 8.3 convert_element_type.167
  1062.9 38.6 %fusion.10 = f32[5,1280,20,64]{1,3,2,0:T(8,128)} fusion(bf16[5,128,20,64]{1,3,2,0:T(8,128)(2,1)S(1)} %copy-done.12, f32[5,20,128,1280]{3,2,1,0:T(8,128)} %get-tuple-element.169, f32[5,20,128]{2,1,0:T(8,128)S(1)} %copy-done.32, pred[5,128,1280]{2,1,0:T(8,128)(4,1)S(1)} %copy-done.6), kind=kOutput, calls=%fused_computation.30 | convolution fusion | flops 2162688000 | bytes 100812800 | tf_op jit(solution)/shard_map/bhqk,bqhd->bkhd/dot_general | solution.py:221
  1101.5 53.5 %copy.241 = f32[5,1280,20,64]{3,2,1,0:T(8,128)} copy(f32[5,1280,20,64]{1,3,2,0:T(8,128)} %fusion.10) | data formatting | bytes 65536000 | tf_op jit(solution)/shard_map/reshape | solution.py:233
  1155.0 57.4 %reshape.926 = f32[50,128,1280]{2,1,0:T(8,128)} reshape(f32[5,1280,20,64]{3,2,1,0:T(8,128)} %copy.241) | data formatting | bytes 65536000 | tf_op jit(solution)/shard_map/reshape | solution.py:233
  1212.4 6.1 broadcast.941.clone
  1218.5 64.8 %scatter_fusion.1 = f32[20,128,1280]{2,1,0:T(8,128)} fusion(f32[20,128,1280]{2,1,0:T(8,128)} %broadcast.941.clone, s32[50]{0:T(128)S(1)} %copy-done.55, f32[50,128,1280]{2,1,0:T(8,128)} %reshape.926), kind=kCustom, calls=%fused_computation.13 | custom fusion | flops 8192000 | bytes 98304200 | tf_op jit(solution)/shard_map/scatter-add | solution.py:233
  1283.3 8.3 convert_element_type.172
  1293.6 2.9 reshape.789
  1296.5 26.3 fusion.23
  1323.1 4.8 copy.224
  1331.1 31.7 %fusion.14 = f32[1280,10240]{1,0:T(8,128)} fusion(bf16[640,5120]{1,0:T(8,128)(2,1)} %multiply_convert_fusion.1, bf16[640,5120]{1,0:T(8,128)(2,1)} %get-tuple-element.148, f32[640,1280]{1,0:T(8,128)S(1)} %copy-done.1, f32[640]{0:T(1024)S(1)} %copy-done.23), kind=kOutput, calls=%fused_computation.43 | convolution fusion | flops 16805068800 | bytes 68815360 | tf_op jit(solution)/shard_map/td,tc->dc/dot_general | solution.py:190
  1362.8 55.9 %concatenate.27 = f32[1280,10248]{1,0:T(8,128)} concatenate(f32[1280,10240]{1,0:T(8,128)} %fusion.14, f32[1280,4]{1,0:T(8,128)} %reshape.794, f32[1280,4]{1,0:T(8,128)} %reshape.795), dimensions={1} | concatenate | bytes 104939520 | tf_op jit(solution)/shard_map/concatenate | solution.py:192
  1418.8 6.9 fusion.27
  1425.6 2.9 copy.243
  1432.6 6.1 fusion.17
  1438.8 4.5 copy.245
  1443.3 14.7 convolution_bitcast_fusion
  1457.9 60.2 %concatenate.26 = f32[1280,5123]{0,1:T(8,128)} concatenate(f32[1280,3840]{0,1:T(8,128)} %convolution_bitcast_fusion, f32[1280,1280]{0,1:T(8,128)} %fusion.27, f32[1280,1]{0,1:T(1,128)S(1)} %add.198, f32[1280,1]{0,1:T(1,128)S(1)} %stack.40, f32[1280,1]{0,1:T(1,128)S(1)} %stack.41), dimensions={1} | concatenate | bytes 52459520 | tf_op jit(solution)/shard_map/concatenate | solution.py:273
  1519.6 17.0 fusion.67
  1537.2 42.5 %psum.14 = f32[]{:T(128)} all-reduce(f32[]{:T(128)} %get-tuple-element.114), channel_id=1, replica_groups=mesh['dp'=8,'fsdp'=4] {'dp','fsdp'}, use_global_device_ids=true, to_apply=%region_9.10 | all-reduce | flops 1 | bytes 8 | tf_op jit(solution)/shard_map/psum | solution.py:160
  1581.1 13.7 convolution_add_fusion
  1594.8 1048.5 %all-reduce.5.cloned.1.call-done = (f32[1280,5123]{0,1:T(8,128)}, f32[1280,10248]{1,0:T(8,128)}) async-done(((f32[1280,5123]{0,1:T(8,128)}, f32[1280,10248]{1,0:T(8,128)}), (f32[1280,5123]{0,1:T(8,128)}, f32[1280,10248]{1,0:T(8,128)})) %all-reduce.5.cloned.1.call-update) | async-done | bytes 78699536
  2643.3 3.3 fusion.66
  2656.5 273.8 %reduce-scatter.9.cloned.1.call-done = f32[160,1280]{1,0:T(8,128)} async-done(((f32[5120,1280]{1,0:T(8,128)}), f32[160,1280]{1,0:T(8,128)}) %reduce-scatter.9.cloned.1.call-update) | async-done | bytes 819216 | tf_op jit(solution)/shard_map/reduce_scatter | solution.py:195
  (274 shorter events, 63.2 us)
Async XLA Ops:
  7.2 88.3 %all-gather.9.cloned.1.call-start = ((), (), s32[]{:S(2)}) async-start(), calls=%async_computation.3 | async-start | bytes 10137600 | tf_op jit(solution)/shard_map/all_gather | solution.py:76
  9.0 261.1 %all-gather.11.cloned.1.call-start = ((), (), s32[]{:S(2)}) async-start(), calls=%async_computation.4 | async-start | bytes 8192000 | tf_op jit(solution)/shard_map/all_gather | solution.py:96
  106.6 3.8 copy-start.2
  111.8 272.1 %all-gather.13.cloned.1.call-start = ((), (), s32[]{:S(2)}) async-start(), calls=%async_computation.5 | async-start | bytes 8192000 | tf_op jit(solution)/shard_map/all_gather | solution.py:95
  141.9 9.0 copy-start.41
  141.9 122.9 %copy-start.35 = (f32[1280]{0:T(1024)}, f32[1280]{0:T(1024)S(1)}, u32[]{:S(2)}) copy-start(f32[1280]{0:T(1024)S(1)} %get-tuple-element.116) | copy-start | bytes 15364
  147.1 3.8 copy-start.7
  150.5 6.9 copy-start.28
  150.9 6.5 copy-start.30
  150.9 7.2 copy-start.33
  150.9 7.2 copy-start.34
  157.4 2.5 copy-start.52
  157.4 4.3 copy-start.62
  157.4 425.8 %all-gather.15.cloned.1.call-start = ((), (), s32[]{:S(2)}) async-start(), calls=%async_computation.6 | async-start | bytes 3379200 | tf_op jit(solution)/shard_map/all_gather | solution.py:77
  158.0 433.0 %all-gather.17.cloned.1.call-start = ((), (), s32[]{:S(2)}) async-start(), calls=%async_computation.7 | async-start | bytes 27033600 | tf_op jit(solution)/shard_map/all_gather | solution.py:138
  159.0 471.8 %all-gather.19.cloned.1.call-start = ((), (), s32[]{:S(2)}) async-start(), calls=%async_computation.8 | async-start | bytes 13516800 | tf_op jit(solution)/shard_map/all_gather | solution.py:154
  159.6 1266.0 %reduce-scatter.11.cloned.1.call-start = ((), (), s32[]{:S(2)}) async-start(), calls=%async_computation.10 | async-start | bytes 8192000
  162.4 10.9 copy-start.59
  162.4 11.1 copy-start.60
  266.3 282.5 %copy-start.5 = (pred[5,128,1280]{2,1,0:T(8,128)(4,1)}, pred[5,128,1280]{2,1,0:T(8,128)(4,1)S(1)}, u32[]{:S(2)}) copy-start(pred[5,128,1280]{2,1,0:T(8,128)(4,1)S(1)} %broadcast_select_fusion) | copy-start | bytes 2457604
  270.1 227.2 %copy-start.9 = (bf16[5,128,20,64]{1,0,3,2:T(8,128)(2,1)}, bf16[5,128,20,64]{1,0,3,2:T(8,128)(2,1)S(1)}, u32[]{:S(2)}) copy-start(bf16[5,128,20,64]{1,0,3,2:T(8,128)(2,1)S(1)} %reshape.781) | copy-start | bytes 4915204
  583.2 5.4 copy-start.20
  583.3 5.4 copy-start.18
  583.3 5.4 copy-start.37
  590.3 131.2 %copy-start = (f32[640,1280]{1,0:T(8,128)}, f32[640,1280]{1,0:T(8,128)S(1)}, u32[]{:S(2)}) copy-start(f32[640,1280]{1,0:T(8,128)S(1)} %get-tuple-element.127) | copy-start | bytes 9830404
  590.3 131.2 %copy-start.22 = (f32[640]{0:T(1024)}, f32[640]{0:T(1024)S(1)}, u32[]{:S(2)}) copy-start(f32[640]{0:T(1024)S(1)} %add_rsqrt_fusion.4) | copy-start | bytes 7684
  591.0 27.2 copy-start.40
  591.0 27.2 copy-start.43
  630.8 13.2 copy-start.36
  644.1 1.9 copy-start.13
  644.1 1.9 copy-start.46
  644.1 1.9 copy-start.53
  653.6 1.7 copy-start.16
  656.0 29.7 %copy-start.25 = (bf16[640,1280]{1,0:T(8,128)(2,1)}, bf16[640,1280]{1,0:T(8,128)(2,1)S(1)}, u32[]{:S(2)}) copy-start(bf16[640,1280]{1,0:T(8,128)(2,1)S(1)} %multiply_convert_fusion.5) | copy-start | bytes 4915204
  685.7 9.2 copy-start.54
  694.9 26.7 copy-start.38
  694.9 26.7 copy-start.45
  721.6 5.6 copy-start.4
  727.2 1.7 copy-start.14
  727.2 3.7 copy-start.61
  737.6 4.6 copy-start.6
  737.6 4.6 copy-start.32
  742.2 55.0 %copy-start.11 = (bf16[5,128,20,64]{1,3,2,0:T(8,128)(2,1)}, bf16[5,128,20,64]{1,3,2,0:T(8,128)(2,1)S(1)}, u32[]{:S(2)}) copy-start(bf16[5,128,20,64]{1,3,2,0:T(8,128)(2,1)S(1)} %copy.221) | copy-start | bytes 4915204
  797.1 52.9 %copy-start.10 = (bf16[5,128,20,64]{1,0,3,2:T(8,128)(2,1)S(1)}, bf16[5,128,20,64]{1,0,3,2:T(8,128)(2,1)}, u32[]{:S(2)}) copy-start(bf16[5,128,20,64]{1,0,3,2:T(8,128)(2,1)} %copy-done.9) | copy-start | bytes 4915204
  981.8 6.1 copy-start.55
  1061.5 377.2 %reduce-scatter.13.cloned.1.call-start = ((), (), s32[]{:S(2)}) async-start(), calls=%async_computation.11 | async-start | bytes 8192000
  1291.6 2.0 copy-start.17
  1291.6 1351.7 %all-reduce.5.cloned.1.call-start = ((), (), s32[]{:S(2)}) async-start(), calls=%async_computation.12 | async-start | bytes 158679040
  1323.1 5.0 copy-start.48
  1323.1 5.0 copy-start.47
  1323.1 5.0 copy-start.51
  1323.1 6.5 copy-start.50
  1323.1 8.0 copy-start.1
  1323.1 8.0 copy-start.23
  1362.8 55.9 %copy-start.21 = (bf16[5,128,20,64]{1,0,3,2:T(8,128)(2,1)S(1)}, bf16[5,128,20,64]{1,0,3,2:T(8,128)(2,1)}, u32[]{:S(2)}) copy-start(bf16[5,128,20,64]{1,0,3,2:T(8,128)(2,1)} %copy-done.20) | copy-start | bytes 4915204
  1425.6 2.9 copy-start.42
  1428.5 1.9 copy-start.8
  1428.5 1.9 copy-start.31
  1429.0 3.6 slice-start
  1430.4 2.2 slice-start.1
  1438.7 19.2 copy-start.24
  1438.7 4.5 copy-start.19
  1518.2 1412.2 %reduce-scatter.9.cloned.1.call-start = ((), (), s32[]{:S(2)}) async-start(), calls=%async_computation.9 | async-start | bytes 27033600 | tf_op jit(solution)/shard_map/reduce_scatter | solution.py:195
  1536.5 44.5 %copy-start.15 = (f32[640,1280]{1,0:T(8,128)S(1)}, f32[640,1280]{1,0:T(8,128)}, u32[]{:S(2)}) copy-start(f32[640,1280]{1,0:T(8,128)} %copy-done.14) | copy-start | bytes 9830404
  (11 other events, 13.9 us)
Sparse Core Ops, SparseCore 0:
  11.5 83.8 all-gather.8
  111.9 46.6 all-gather.10
  160.2 51.7 all-gather.12
  214.7 58.7 all-gather.14
  276.8 157.2 all-gather.16
  436.8 97.6 all-gather.18
  1061.7 58.2 reduce-scatter.10
  1291.7 59.9 reduce-scatter.12
  1518.3 1124.9 all-reduce.4
  2646.0 284.3 reduce-scatter.8
where the time goes:
time: 2960 us; the launch traced here: 2940 us
  waiting for transfers between devices  1410 us (48%)
  local copies, waits for them, and re-layouts  656 us (22%)
  matrix products  402 us (14%)
  other arithmetic  292 us (10%)
  blocking collectives  160 us (5%)
    unnamed x13, waiting for transfers between devices  1050 us
    reduce_scatter x1, waiting for transfers between devices, local(): lax.psum_scatter(jnp.einsum('tf,te->fe', lefts, g_down, preferred_element...  274 us
    reshape x2, local copies, waits for them, and re-layouts, local(): g_value_rows.reshape(blocks_dev * DEPTH, BLOCK, D)  111 us
    reshape x2, local copies, waits for them, and re-layouts, local(): g_key_rows.reshape(blocks_dev * DEPTH, BLOCK, D)  111 us
    reshape x2, local copies, waits for them, and re-layouts, local(): key_group.reshape(group_blocks, BLOCK, D)[safe_paths]  93.3 us
    reshape x2, local copies, waits for them, and re-layouts, local(): value_group.reshape(group_blocks, BLOCK, D)[safe_paths]  93.2 us
    psum x2, blocking collectives, local(): lax.psum((jnp.sum(mask_f), loss_local), ('dp', 'fsdp'))  92.9 us
    all_gather x1, waiting for transfers between devices, local(): piece_qkv = lax.all_gather(qkv_local, ('dp', 'fsdp'), axis=0, tiled=True)  86.4 us
  transfers between devices with their start and end apart: 10, of which 3 were waited for; matrix products, arithmetic and copies ran while one was open for 28% of the time, Pallas kernels for 0%

commit v1 on v0

--- a/solution.py
+++ b/solution.py
@@ -73,8 +73,16 @@
     mask_f = valid_mask.astype(jnp.float32)
     qkv_local = jnp.concatenate((w_query, w_key, w_value), axis=1)
     scal_width_local = jnp.stack((qk_scale, attn_rate, mlp_rate), axis=1)
-    piece_qkv = lax.all_gather(qkv_local, ("dp", "fsdp"), axis=0, tiled=True)
-    piece_out = lax.all_gather(w_out, ("dp", "fsdp"), axis=0, tiled=True)
+
+    def meshes_state(vec, local_x, a_name):
+        next_value = jnp.split(
+            lax.all_gather(jnp.concatenate([vec, local_x], axis=1), a_name, axis=0, tiled=True),
+            [vec.shape[1]],
+            axis=1,
+        )
+        return next_value
+
+    piece_qkv, piece_out = meshes_state(qkv_local, w_out, ("dp", "fsdp"))
     piece_scal = lax.all_gather(scal_width_local, ("dp", "fsdp"), axis=0, tiled=True)
     lefts = states
     total = jnp.dot(lefts, piece_qkv, preferred_element_type=jnp.float32)

time: 2960 us -> 2980 us (level)
  transfers between devices with their start and end apart: 10 -> 10, of which waited for: 3 -> 3; matrix products, arithmetic and copies ran while one was open for 28% -> 30% of each run, Pallas kernels for 0% -> 0%
where the time goes in v1:
time: 2980 us; the launch traced here: 2950 us
  waiting for transfers between devices  1420 us (48%)
  local copies, waits for them, and re-layouts  651 us (22%)
  matrix products  402 us (13%)
  other arithmetic  298 us (10%)
  blocking collectives  160 us (5%)
    unnamed x13, waiting for transfers between devices  1050 us
    reduce_scatter x1, waiting for transfers between devices, local(): lax.psum_scatter(jnp.einsum('tf,te->fe', lefts, g_down, preferred_element...  274 us
    reshape x2, local copies, waits for them, and re-layouts, local(): g_value_rows.reshape(blocks_dev * DEPTH, BLOCK, D)  111 us
    reshape x2, local copies, waits for them, and re-layouts, local(): g_key_rows.reshape(blocks_dev * DEPTH, BLOCK, D)  111 us
    all_gather x1, waiting for transfers between devices, meshes_state(): lax.all_gather(jnp.concatenate([vec, local_x], axis=1), a_name, axis=0, t...  100 us
    reshape x2, local copies, waits for them, and re-layouts, local(): value_group.reshape(group_blocks, BLOCK, D)[safe_paths]  93.2 us
    reshape x2, local copies, waits for them, and re-layouts, local(): key_group.reshape(group_blocks, BLOCK, D)[safe_paths]  92.8 us
    psum x2, blocking collectives, local(): lax.psum((jnp.sum(mask_f), loss_local), ('dp', 'fsdp'))  92.4 us
  transfers between devices with their start and end apart: 10, of which 3 were waited for; matrix products, arithmetic and copies ran while one was open for 30% of the time, Pallas kernels for 0%

profile of v1, /device:TPU:14, one launch (start us, length us, event | category | flops | bytes accessed | tf_op | source)
XLA Modules:
  0.0 2953.9 jit_solution(10457363003389133343)
XLA Ops:
  9.1 100.3 %all-gather.9.cloned.1.call-done = bf16[1280,5120]{1,0:T(8,128)(2,1)} async-done(((bf16[40,5120]{1,0:T(8,128)(2,1)}), bf16[1280,5120]{1,0:T(8,128)(2,1)}) %all-gather.9.cloned.1.call-update) | async-done | bytes 13107216 | tf_op jit(solution)/shard_map/all_gather | solution.py:79
  109.5 11.0 fusion.18
  120.5 3.8 copy-done.2
  125.7 29.6 %all-gather = bf16[32,40,3]{1,2,0:T(4,128)(2,1)S(1)} all-gather(bf16[1,40,3]{1,2,0:T(4,128)(2,1)S(1)} %maximum_bitcast_fusion.1), channel_id=1, replica_groups=mesh['dp'=8,'fsdp'=4] {'dp','fsdp'}, dimensions={0}, use_global_device_ids=true | all-gather | bytes 7920 | tf_op jit(solution)/shard_map/all_gather | solution.py:86
  156.1 5.1 slice_multiply_fusion.1
  161.2 3.4 reduce_sum.198
  165.0 6.5 multiply_convert_fusion.7
  188.5 38.1 %all-gather.1 = bf16[32,40,8]{1,2,0:T(8,128)(2,1)S(1)} all-gather(bf16[1,40,8]{1,2,0:T(8,128)(2,1)S(1)} %maximum_bitcast_fusion), channel_id=1, replica_groups=mesh['dp'=8,'fsdp'=4] {'dp','fsdp'}, dimensions={0}, use_global_device_ids=true | all-gather | bytes 21120 | tf_op jit(solution)/shard_map/all_gather | solution.py:147
  229.1 50.5 %psum.15 = f32[]{:T(128)} all-reduce(f32[]{:T(128)} %get-tuple-element.167), channel_id=1, replica_groups=mesh['dp'=8,'fsdp'=4] {'dp','fsdp'}, use_global_device_ids=true, to_apply=%region_11.12 | all-reduce | flops 1 | bytes 8 | tf_op jit(solution)/shard_map/psum | solution.py:168
  281.1 3.8 reshape.781
  284.9 9.9 copy.194
  294.8 10.6 gather_fusion.9
  305.4 46.4 %reshape.933 = bf16[5,1280,20,64]{3,2,1,0:T(8,128)(2,1)} reshape(bf16[50,128,1280]{2,1,0:T(8,128)(2,1)} %gather_fusion.9) | data formatting | bytes 32768000 | tf_op jit(solution)/shard_map/reshape | solution.py:116
  351.8 46.9 %copy.213 = bf16[5,1280,20,64]{1,3,2,0:T(8,128)(2,1)} copy(bf16[5,1280,20,64]{3,2,1,0:T(8,128)(2,1)} %reshape.933) | data formatting | bytes 32768000 | tf_op jit(solution)/shard_map/reshape | solution.py:116
  398.6 9.6 copy.209
  408.2 10.6 gather_fusion.11
  418.8 46.3 %reshape.934 = bf16[5,1280,20,64]{3,2,1,0:T(8,128)(2,1)} reshape(bf16[50,128,1280]{2,1,0:T(8,128)(2,1)} %gather_fusion.11) | data formatting | bytes 32768000 | tf_op jit(solution)/shard_map/reshape | solution.py:113
  465.1 46.6 %copy.212 = bf16[5,1280,20,64]{1,3,2,0:T(8,128)(2,1)} copy(bf16[5,1280,20,64]{3,2,1,0:T(8,128)(2,1)} %reshape.934) | data formatting | bytes 32768000 | tf_op jit(solution)/shard_map/reshape | solution.py:113
  511.7 29.2 select_reduce_fusion
  540.9 20.8 fusion.1
  561.8 30.6 %fusion.39 = bf16[5,128,20,64]{1,3,2,0:T(8,128)(2,1)S(1)} fusion(bf16[5,1280,20,64]{1,3,2,0:T(8,128)(2,1)} %copy.213, f32[5,20,128,1280]{3,2,1,0:T(8,128)} %get-tuple-element.169, f32[5,20,128]{2,1,0:T(8,128)S(1)} %fusion.1, f32[5,20,128]{2,1,0:T(8,128)S(1)} %get-tuple-element.168, pred[5,128,1280]{2,1,0:T(8,128)(4,1)S(1)} %broadcast_select_fusion), kind=kOutput, calls=%fused_computation.111 | convolution fusion | flops 2179891200 | bytes 84480000 | tf_op jit(solution)/shard_map/bhqk,bkhd->bqhd/dot_general | solution.py:135
  593.9 5.3 multiply_reduce_fusion.14
  601.6 27.2 fusion.70
  628.9 12.5 multiply_convert_fusion.3
  641.4 13.2 multiply_reduce_fusion.12
  656.5 2.9 multiply_reduce_fusion.9
  659.5 4.6 multiply_reduce_fusion.3
  666.5 29.6 %multiply_reduce_fusion.1 = (f32[5120]{0:T(1024)}, f32[5120]{0:T(1024)}, f32[640,5120]{1,0:T(8,128)}, bf16[640,5120]{1,0:T(8,128)(2,1)}) fusion(f32[640,10240]{1,0:T(8,128)} %fusion.70, f32[5120]{0:T(1024)S(1)} %copy-done.40, f32[5120]{0:T(1024)S(1)} %copy-done.43, bf16[640,1280]{1,0:T(8,128)(2,1)S(1)} %multiply_convert_fusion.5, ...), kind=kOutput, calls=%fused_computation.33 | convolution fusion | flops 8457410560 | bytes 60702720 | tf_op jit(solution)/shard_map/te,fe->tf/dot_general | solution.py:175
  696.1 9.1 multiply_convert_fusion.1
  705.3 26.6 multiply_reduce_fusion.7
  731.9 5.6 multiply_reduce_fusion.4
  740.4 4.2 convolution_convert_fusion
  744.7 4.3 reshape.935
  749.0 4.6 copy.221
  753.6 55.0 %multiply_reduce_fusion = (f32[5,20,128]{2,1,0:T(8,128)}, f32[5,20,128,1280]{3,2,1,0:T(8,128)}) fusion(f32[5,20,128,1280]{3,2,1,0:T(8,128)} %get-tuple-element.169, f32[5,20,128]{2,1,0:T(8,128)S(1)} %copy-done.32, pred[5,128,1280]{2,1,0:T(8,128)(4,1)S(1)} %copy-done.6, bf16[5,128,20,64]{1,3,2,0:T(8,128)(2,1)S(1)} %copy.221, bf16[5,1280,20,64]{1,3,2,0:T(8,128)(2,1)} %copy.213), kind=kOutput, calls=%fused_computation.16 | convolution fusion | flops 2179059200 | bytes 150016000 | tf_op jit(solution)/shard_map/bqhd,bkhd->bhqk/dot_general | solution.py:220
  808.6 52.9 %multiply_convert_fusion = bf16[5,20,128,1280]{3,2,1,0:T(8,128)(2,1)} fusion(f32[5,20,128,1280]{3,2,1,0:T(8,128)} %get-tuple-element.177, f32[5,20,128,1280]{3,2,1,0:T(8,128)} %get-tuple-element.169, f32[5,20,128]{2,1,0:T(8,128)} %get-tuple-element.176, f32[5,20,128]{2,1,0:T(8,128)S(1)} %copy-done.32, pred[5,128,1280]{2,1,0:T(8,128)(4,1)S(1)} %copy-done.6), kind=kLoop, calls=%fused_computation.15 | loop fusion | flops 98304000 | bytes 164761600 | tf_op jit(solution)/shard_map/convert_element_type | solution.py:222
  861.5 20.9 multiply_bitcast_fusion
  882.4 53.4 %copy.240 = f32[5,1280,20,64]{3,2,1,0:T(8,128)} copy(f32[5,1280,20,64]{1,3,2,0:T(8,128)} %multiply_bitcast_fusion) | data formatting | bytes 65536000 | tf_op jit(solution)/shard_map/reshape | solution.py:236
  935.8 57.4 %reshape.925 = f32[50,128,1280]{2,1,0:T(8,128)} reshape(f32[5,1280,20,64]{3,2,1,0:T(8,128)} %copy.240) | data formatting | bytes 65536000 | tf_op jit(solution)/shard_map/reshape | solution.py:236
  993.2 6.1 broadcast.941.clone.1
  999.3 65.4 %scatter_fusion = f32[20,128,1280]{2,1,0:T(8,128)} fusion(f32[20,128,1280]{2,1,0:T(8,128)} %broadcast.941.clone.1, s32[50]{0:T(128)S(1)} %copy-done.55, f32[50,128,1280]{2,1,0:T(8,128)} %reshape.925), kind=kCustom, calls=%fused_computation.12 | custom fusion | flops 8192000 | bytes 98304200 | tf_op jit(solution)/shard_map/scatter-add | solution.py:236
  1064.7 8.4 convert_element_type.167
  1074.5 39.3 %fusion.10 = f32[5,1280,20,64]{1,3,2,0:T(8,128)} fusion(bf16[5,128,20,64]{1,3,2,0:T(8,128)(2,1)S(1)} %copy-done.12, f32[5,20,128,1280]{3,2,1,0:T(8,128)} %get-tuple-element.169, f32[5,20,128]{2,1,0:T(8,128)S(1)} %copy-done.32, pred[5,128,1280]{2,1,0:T(8,128)(4,1)S(1)} %copy-done.6), kind=kOutput, calls=%fused_computation.30 | convolution fusion | flops 2162688000 | bytes 100812800 | tf_op jit(solution)/shard_map/bhqk,bqhd->bkhd/dot_general | solution.py:229
  1113.8 53.4 %copy.241 = f32[5,1280,20,64]{3,2,1,0:T(8,128)} copy(f32[5,1280,20,64]{1,3,2,0:T(8,128)} %fusion.10) | data formatting | bytes 65536000 | tf_op jit(solution)/shard_map/reshape | solution.py:241
  1167.3 57.4 %reshape.926 = f32[50,128,1280]{2,1,0:T(8,128)} reshape(f32[5,1280,20,64]{3,2,1,0:T(8,128)} %copy.241) | data formatting | bytes 65536000 | tf_op jit(solution)/shard_map/reshape | solution.py:241
  1224.7 6.1 broadcast.941.clone
  1230.8 64.8 %scatter_fusion.1 = f32[20,128,1280]{2,1,0:T(8,128)} fusion(f32[20,128,1280]{2,1,0:T(8,128)} %broadcast.941.clone, s32[50]{0:T(128)S(1)} %copy-done.55, f32[50,128,1280]{2,1,0:T(8,128)} %reshape.926), kind=kCustom, calls=%fused_computation.13 | custom fusion | flops 8192000 | bytes 98304200 | tf_op jit(solution)/shard_map/scatter-add | solution.py:241
  1295.5 8.4 convert_element_type.172
  1309.7 25.3 fusion.28
  1335.4 4.9 copy.224
  1343.5 31.9 %fusion.16 = f32[1280,10240]{1,0:T(8,128)} fusion(bf16[640,5120]{1,0:T(8,128)(2,1)} %multiply_convert_fusion.1, bf16[640,5120]{1,0:T(8,128)(2,1)} %get-tuple-element.148, f32[640,1280]{1,0:T(8,128)S(1)} %copy-done.1, f32[640]{0:T(1024)S(1)} %copy-done.23), kind=kOutput, calls=%fused_computation.45 | convolution fusion | flops 16805068800 | bytes 68815360 | tf_op jit(solution)/shard_map/td,tc->dc/dot_general | solution.py:198
  1375.3 56.2 %concatenate.32 = f32[1280,10248]{1,0:T(8,128)} concatenate(f32[1280,10240]{1,0:T(8,128)} %fusion.16, f32[1280,4]{1,0:T(8,128)} %reshape.794, f32[1280,4]{1,0:T(8,128)} %reshape.795), dimensions={1} | concatenate | bytes 104939520 | tf_op jit(solution)/shard_map/concatenate | solution.py:200
  1431.5 6.9 fusion.35
  1438.5 3.7 copy.243
  1446.5 7.1 fusion.22
  1453.7 4.1 copy.245
  1457.8 14.7 convolution_bitcast_fusion
  1472.4 60.2 %concatenate.31 = f32[1280,5123]{0,1:T(8,128)} concatenate(f32[1280,3840]{0,1:T(8,128)} %convolution_bitcast_fusion, f32[1280,1280]{0,1:T(8,128)} %fusion.35, f32[1280,1]{0,1:T(1,128)S(1)} %add.198, f32[1280,1]{0,1:T(1,128)S(1)} %stack.40, f32[1280,1]{0,1:T(1,128)S(1)} %stack.41), dimensions={1} | concatenate | bytes 52459520 | tf_op jit(solution)/shard_map/concatenate | solution.py:281
  1534.1 17.0 fusion.74
  1551.7 42.0 %psum.14 = f32[]{:T(128)} all-reduce(f32[]{:T(128)} %get-tuple-element.114), channel_id=1, replica_groups=mesh['dp'=8,'fsdp'=4] {'dp','fsdp'}, use_global_device_ids=true, to_apply=%region_9.10 | all-reduce | flops 1 | bytes 8 | tf_op jit(solution)/shard_map/psum | solution.py:168
  1595.1 13.8 convolution_add_fusion
  1608.9 1049.5 %all-reduce.5.cloned.1.call-done = (f32[1280,5123]{0,1:T(8,128)}, f32[1280,10248]{1,0:T(8,128)}) async-done(((f32[1280,5123]{0,1:T(8,128)}, f32[1280,10248]{1,0:T(8,128)}), (f32[1280,5123]{0,1:T(8,128)}, f32[1280,10248]{1,0:T(8,128)})) %all-reduce.5.cloned.1.call-update) | async-done | bytes 78699536
  2658.4 3.3 fusion.73
  2671.7 273.8 %reduce-scatter.9.cloned.1.call-done = f32[160,1280]{1,0:T(8,128)} async-done(((f32[5120,1280]{1,0:T(8,128)}), f32[160,1280]{1,0:T(8,128)}) %reduce-scatter.9.cloned.1.call-update) | async-done | bytes 819216 | tf_op jit(solution)/shard_map/reduce_scatter | solution.py:203
  (273 shorter events, 63.4 us)
Async XLA Ops:
  7.2 102.3 %all-gather.9.cloned.1.call-start = ((), (), s32[]{:S(2)}) async-start(), calls=%async_computation.3 | async-start | bytes 13516800 | tf_op jit(solution)/shard_map/all_gather | solution.py:79
  9.1 275.8 %all-gather.11.cloned.1.call-start = ((), (), s32[]{:S(2)}) async-start(), calls=%async_computation.4 | async-start | bytes 8192000 | tf_op jit(solution)/shard_map/all_gather | solution.py:104
  120.5 3.8 copy-start.2
  125.7 273.0 %all-gather.13.cloned.1.call-start = ((), (), s32[]{:S(2)}) async-start(), calls=%async_computation.5 | async-start | bytes 8192000 | tf_op jit(solution)/shard_map/all_gather | solution.py:103
  156.1 8.9 copy-start.41
  156.1 123.5 %copy-start.35 = (f32[1280]{0:T(1024)}, f32[1280]{0:T(1024)S(1)}, u32[]{:S(2)}) copy-start(f32[1280]{0:T(1024)S(1)} %get-tuple-element.116) | copy-start | bytes 15364
  161.2 10.3 copy-start.7
  164.6 6.9 copy-start.28
  165.0 6.5 copy-start.30
  171.5 3.1 copy-start.52
  171.5 4.9 copy-start.61
  171.5 430.1 %all-gather.15.cloned.1.call-start = ((), (), s32[]{:S(2)}) async-start(), calls=%async_computation.6 | async-start | bytes 27033600 | tf_op jit(solution)/shard_map/all_gather | solution.py:146
  173.7 14.3 copy-start.59
  173.7 14.5 copy-start.60
  173.7 467.7 %all-gather.17.cloned.1.call-start = ((), (), s32[]{:S(2)}) async-start(), calls=%async_computation.7 | async-start | bytes 13516800 | tf_op jit(solution)/shard_map/all_gather | solution.py:162
  174.3 1264.2 %reduce-scatter.11.cloned.1.call-start = ((), (), s32[]{:S(2)}) async-start(), calls=%async_computation.10 | async-start | bytes 8192000
  281.1 280.7 %copy-start.5 = (pred[5,128,1280]{2,1,0:T(8,128)(4,1)}, pred[5,128,1280]{2,1,0:T(8,128)(4,1)S(1)}, u32[]{:S(2)}) copy-start(pred[5,128,1280]{2,1,0:T(8,128)(4,1)S(1)} %broadcast_select_fusion) | copy-start | bytes 2457604
  284.9 226.8 %copy-start.9 = (bf16[5,128,20,64]{1,0,3,2:T(8,128)(2,1)}, bf16[5,128,20,64]{1,0,3,2:T(8,128)(2,1)S(1)}, u32[]{:S(2)}) copy-start(bf16[5,128,20,64]{1,0,3,2:T(8,128)(2,1)S(1)} %reshape.781) | copy-start | bytes 4915204
  593.8 5.4 copy-start.20
  593.9 5.4 copy-start.18
  593.9 5.4 copy-start.37
  599.2 1.7 copy-start.3
  599.2 1.7 copy-start.44
  600.9 131.0 %copy-start = (f32[640,1280]{1,0:T(8,128)}, f32[640,1280]{1,0:T(8,128)S(1)}, u32[]{:S(2)}) copy-start(f32[640,1280]{1,0:T(8,128)S(1)} %get-tuple-element.127) | copy-start | bytes 9830404
  600.9 131.0 %copy-start.22 = (f32[640]{0:T(1024)}, f32[640]{0:T(1024)S(1)}, u32[]{:S(2)}) copy-start(f32[640]{0:T(1024)S(1)} %add_rsqrt_fusion.4) | copy-start | bytes 7684
  601.6 27.2 copy-start.40
  601.6 27.2 copy-start.43
  641.4 13.2 copy-start.36
  654.6 1.9 copy-start.13
  654.6 1.9 copy-start.46
  654.6 1.9 copy-start.53
  664.1 1.7 copy-start.16
  666.5 29.7 %copy-start.25 = (bf16[640,1280]{1,0:T(8,128)(2,1)}, bf16[640,1280]{1,0:T(8,128)(2,1)S(1)}, u32[]{:S(2)}) copy-start(bf16[640,1280]{1,0:T(8,128)(2,1)S(1)} %multiply_convert_fusion.5) | copy-start | bytes 4915204
  696.1 9.1 copy-start.54
  705.3 26.6 copy-start.38
  705.3 26.6 copy-start.45
  731.9 5.6 copy-start.4
  749.0 4.6 copy-start.6
  749.0 4.6 copy-start.32
  753.6 55.0 %copy-start.11 = (bf16[5,128,20,64]{1,3,2,0:T(8,128)(2,1)}, bf16[5,128,20,64]{1,3,2,0:T(8,128)(2,1)S(1)}, u32[]{:S(2)}) copy-start(bf16[5,128,20,64]{1,3,2,0:T(8,128)(2,1)S(1)} %copy.221) | copy-start | bytes 4915204
  808.6 52.9 %copy-start.10 = (bf16[5,128,20,64]{1,0,3,2:T(8,128)(2,1)S(1)}, bf16[5,128,20,64]{1,0,3,2:T(8,128)(2,1)}, u32[]{:S(2)}) copy-start(bf16[5,128,20,64]{1,0,3,2:T(8,128)(2,1)} %copy-done.9) | copy-start | bytes 4915204
  993.2 6.1 copy-start.55
  1073.1 380.6 %reduce-scatter.13.cloned.1.call-start = ((), (), s32[]{:S(2)}) async-start(), calls=%async_computation.11 | async-start | bytes 8192000
  1303.9 2.8 copy-start.49
  1303.9 2.9 copy-start.29
  1303.9 2.9 copy-start.17
  1303.9 291.1 %all-gather.19.cloned.1.call-start = ((), (), s32[]{:S(2)}) async-start(), calls=%async_computation.8 | async-start | bytes 10137600 | tf_op jit(solution)/shard_map/all_gather | solution.py:273
  1306.7 1351.8 %all-reduce.5.cloned.1.call-start = ((), (), s32[]{:S(2)}) async-start(), calls=%async_computation.12 | async-start | bytes 158679040
  1335.4 5.0 copy-start.48
  1335.4 5.0 copy-start.47
  1335.4 5.0 copy-start.51
  1335.4 6.5 copy-start.50
  1335.4 8.0 copy-start.1
  1335.4 8.0 copy-start.23
  1375.3 56.2 %copy-start.21 = (bf16[5,128,20,64]{1,0,3,2:T(8,128)(2,1)S(1)}, bf16[5,128,20,64]{1,0,3,2:T(8,128)(2,1)}, u32[]{:S(2)}) copy-start(bf16[5,128,20,64]{1,0,3,2:T(8,128)(2,1)} %copy-done.20) | copy-start | bytes 4915204
  1431.5 10.7 copy-start.42
  1438.5 5.9 copy-start.8
  1438.5 5.9 copy-start.31
  1442.2 4.3 slice-start
  1444.4 2.2 slice-start.1
  1446.5 11.2 copy-start.19
  1453.7 18.8 copy-start.24
  1532.7 1412.9 %reduce-scatter.9.cloned.1.call-start = ((), (), s32[]{:S(2)}) async-start(), calls=%async_computation.9 | async-start | bytes 27033600 | tf_op jit(solution)/shard_map/reduce_scatter | solution.py:203
  1551.0 44.0 %copy-start.15 = (f32[640,1280]{1,0:T(8,128)S(1)}, f32[640,1280]{1,0:T(8,128)}, u32[]{:S(2)}) copy-start(f32[640,1280]{1,0:T(8,128)} %copy-done.14) | copy-start | bytes 9830404
  (10 other events, 12.6 us)
Sparse Core Ops, SparseCore 0:
  11.4 97.9 all-gather.8
  125.8 46.9 all-gather.10
  174.3 51.7 all-gather.12
  229.3 159.0 all-gather.14
  391.2 97.8 all-gather.16
  1073.2 58.5 reduce-scatter.10
  1304.0 59.3 reduce-scatter.12
  1366.9 83.7 all-gather.18
  1532.8 1125.5 all-reduce.4
  2661.2 284.3 reduce-scatter.8
